TPU v7x, 512 devices: a whole 4x4x16 slice. The times are simulated.
512 devices in a mesh: space: 64 (over x, z), node: 4 (over y_hi, core), tm: 2 (over y_lo).
Axes of the slice: x: 4, y: 4 (y_hi: 2, y_lo: 2; y = y_hi * 2 + y_lo), z: 16, core: 2. Of those that a mesh axis runs over, the one named last changes fastest.
Arguments:
- start_old: float32 [2, 512, 128, 256], P('tm', 'space'), may hold values from -4 to 4
- nodes_old: float32 [2, 4, 512, 128, 256], P('tm', 'node', 'space'), may hold values from -4 to 4
Outputs:
- nodes_new: float32 [2, 4, 512, 128, 256], P('tm', 'node', 'space')
- end_new: float32 [2, 512, 128, 256], P('tm', 'space')
All inputs are finite; a program needn't handle non-finite values.
Results may differ from a plain program's by a relative error of at most 0.00002.
Values sent between devices are 32-bit elements; how exact they have to be, the bound alone decides.
A program may use at most 64 MiB of HBM per device.

v0:
```python
import jax
import jax.numpy as jnp
from jax import lax
from jax.sharding import PartitionSpec as P

NODES = 4
PASSES = 4
time_step = 0.25
diffusion = 4.0
reaction = 1.0


def padded_2(block, sides, width):
    for axis, dim in sides:
        count = lax.axis_size(axis)
        forward = [(i, i + 1) for i in range(count - 1)]
        forward.append((count - 1, 0))
        backward = [(target, source) for source, target in forward]
        low = lax.ppermute(
            lax.slice_in_dim(block, block.shape[dim] - width, None, axis=dim), axis, forward
        )
        high = lax.ppermute(lax.slice_in_dim(block, 0, width, axis=dim), axis, backward)
        block = jnp.concatenate([low, block, high], axis=dim)
    return block


def shifted_2(array, axis, by):
    size = lax.axis_size(axis)
    pairs = [(i, i + by) for i in range(size) if 0 <= i + by < size]
    return lax.ppermute(array, axis, pairs)


def collocation(count):
    points = [-0.8611363115940526, -0.3399810435848563, 0.3399810435848563, 0.8611363115940526]
    raw_weights = [0.3478548451374538, 0.6521451548625461, 0.6521451548625461, 0.3478548451374538]
    node_times = [(point + 1.0) / 2.0 for point in points]
    quadrature = [[0.0 for column in range(count)] for target in range(count)]
    for source in range(count):
        coeffs = [1.0]
        scaling = 1.0
        for other in range(count):
            if other != source:
                other_time = node_times[other]
                shifted = [0.0] + coeffs
                for power in range(len(coeffs)):
                    shifted[power] = shifted[power] - other_time * coeffs[power]
                coeffs = shifted
                scaling = scaling * (node_times[source] - other_time)
        for target in range(count):
            target_time = node_times[target]
            integral = 0.0
            for power in range(len(coeffs)):
                integral = integral + coeffs[power] * target_time ** (power + 1) / (power + 1)
            quadrature[target][source] = integral / scaling
    return (node_times, quadrature, [weight / 2.0 for weight in raw_weights])


def neighbour_sum(padded):
    inner = padded[1:-1]
    total = padded[2:] + padded[:-2]
    total = total + jnp.roll(inner, -1, 1) + jnp.roll(inner, 1, 1)
    total = total + jnp.roll(inner, -1, 2) + jnp.roll(inner, 1, 2)
    return total


def forcing(values, padded):
    laplace = neighbour_sum(padded) - 6.0 * values
    return (laplace, diffusion * laplace + reaction * (values - values * values * values))


def on_device(start_old, nodes_old):
    node_times, quadrature, weights = collocation(NODES)
    node_index = lax.axis_index("node")
    node_time = jnp.asarray(node_times, jnp.float32)[node_index]
    weight_table = jnp.asarray(weights, jnp.float32)
    node_weight = weight_table[node_index]
    quad_table = jnp.asarray(quadrature, jnp.float32)
    state_old = nodes_old[0, 0]
    start_state = start_old[0]
    padded = padded_2(state_old, (("space", 0),), 1)
    laplace_old, force_old = forcing(state_old, padded)
    quad_row = quad_table[node_index]
    shard_piece = lax.all_gather(force_old[None], "node", axis=0, tiled=True)
    quad_part = jnp.sum(quad_row[:, None, None, None] * shard_piece, axis=0)
    weight_part = jnp.sum(weight_table[:, None, None, None] * shard_piece, axis=0)
    end_old = start_state + time_step * weight_part
    received = shifted_2(end_old, "tm", 1)
    begin_state = jnp.where(lax.axis_index("tm") == 0, start_state, received)
    implicit = time_step * diffusion * node_time
    right_side = begin_state + time_step * quad_part - implicit * laplace_old
    divisor = 1.0 + 6.0 * implicit
    iterate = state_old
    for step_index in range(PASSES):
        widened = padded_2(iterate, (("space", 0),), 1)
        iterate = (right_side + implicit * neighbour_sum(widened)) / divisor
    padded_new = padded_2(iterate, (("space", 0),), 1)
    laplace_new, force_new = forcing(iterate, padded_new)
    weighted_new = lax.psum(node_weight * force_new, "node")
    end_new = begin_state + time_step * weighted_new
    return (iterate[None, None], end_new[None])


def solution(mesh):
    return jax.shard_map(
        on_device,
        mesh=mesh,
        in_specs=(P("tm", "space", None, None), P("tm", "node", "space", None, None)),
        out_specs=(P("tm", "node", "space", None, None), P("tm", "space", None, None)),
        check_vma=False,
    )
```

profile of v0, /device:TPU:1, one launch (start us, length us, event | category | flops | bytes accessed | tf_op | source)
XLA Modules:
  0.0 228.6 jit_solution(15902153033855880192)
XLA Ops:
  7.2 0.0 copy-start
  7.2 0.0 all-gather.3.cloned.1.call-start
  7.2 1.1 slice_bitcast_fusion.1
  8.3 14.1 %collective-permute-start = (f32[1,128,256]{2,1,0:T(8,128)S(1)}, f32[1,128,256]{2,1,0:T(8,128)S(1)}, u32[]{:S(2)}, u32[]{:S(2)}) collective-permute-start(f32[1,128,256]{2,1,0:T(8,128)S(1)} %get-tuple-element.48), channel_id=1, source_target_pairs={{8,0},{16,8},{24,16},{32,24},{40,32},{48,40},{56,48},{64,56},{72,6... | collective-permute-start | bytes 393224 | tf_op jit(solution)/shard_map/ppermute | solution.py:22
  22.4 1.9 collective-permute-start.1
  24.4 1.4 fusion.63
  25.8 1.9 fusion.62
  27.7 0.0 copy-done
  27.7 0.2 fusion.60
  27.9 0.0 collective-permute-done
  27.9 3.5 %collective-permute-done.1 = f32[1,128,256]{2,1,0:T(8,128)S(1)} collective-permute-done((f32[1,128,256]{2,1,0:T(8,128)S(1)}, f32[1,128,256]{2,1,0:T(8,128)S(1)}, u32[]{:S(2)}, u32[]{:S(2)}) %collective-permute-start.1) | collective-permute-done | bytes 131104 | tf_op jit(solution)/shard_map/ppermute | solution.py:19
  31.5 0.0 copy-start.3
  31.5 2.2 fusion
  33.7 0.0 all-gather.3.cloned.1.call-update
  33.7 0.0 all-reduce.2.cloned.1.call-start
  33.8 0.8 dynamic-slice_bitcast_fusion
  34.5 38.3 %all-gather.3.cloned.1.call-done = f32[32,128,256]{2,1,0:T(8,128)} async-done(((f32[8,128,256]{2,1,0:T(8,128)}), f32[32,128,256]{2,1,0:T(8,128)}) %all-gather.3.cloned.1.call-update) | async-done | bytes 4194320 | tf_op jit(solution)/shard_map/all_gather | solution.py:83
  72.8 0.0 copy-done.3
  72.8 4.1 %multiply_reduce_fusion.1 = (f32[8,128,256]{2,1,0:T(8,128)S(1)}, f32[8,128,256]{2,1,0:T(8,128)}) fusion(f32[4,8,128,256]{3,2,1,0:T(8,128)} %bitcast.30, f32[4]{0:T(128)S(1)} %copy-done.3, f32[4]{0:T(128)S(1)} %dynamic-slice_bitcast_fusion), kind=kLoop, calls=%fused_computation.1 | loop fusion | flops 3670016 | bytes 6291488 | tf_op jit(solution)/shard_map/reduce_sum | solution.py:85
  76.9 0.0 copy-done.2
  76.9 1.1 bitcast_add_fusion
  78.0 2.3 collective-permute-start.2
  80.3 0.7 dynamic_slice.11
  81.0 0.0 copy-done.4
  81.0 0.6 dynamic_slice.10
  82.1 20.7 %collective-permute-done.2 = f32[8,128,256]{2,1,0:T(8,128)S(1)} collective-permute-done((f32[8,128,256]{2,1,0:T(8,128)}, f32[8,128,256]{2,1,0:T(8,128)S(1)}, u32[]{:S(2)}, u32[]{:S(2)}) %collective-permute-start.2) | collective-permute-done | bytes 1048608 | tf_op jit(solution)/shard_map/ppermute | solution.py:30
  102.8 2.5 %add_divide_fusion = (f32[8,128,256]{2,1,0:T(8,128)S(1)}, f32[8,128,256]{2,1,0:T(8,128)S(1)}) fusion(f32[8,128,256]{2,1,0:T(8,128)} %get-tuple-element.7, f32[]{:T(128)S(6)} %add.127, f32[]{:T(128)} %bitcast.6, f32[1,1,8,128,256]{4,3,2,1,0:T(8,128)S(1)} %copy-done, f32[8,128,256]{2,1,0:T(8,128)} %get-tuple-element.3, ...), kind=kLoop, calls=%fused_computation.56 | loop fusion | flops 2621440 | bytes 7340041 | tf_op jit(solution)/shard_map/div | solution.py:95
  105.3 0.2 fusion.55
  105.5 0.2 fusion.58
  105.7 0.4 fusion.56
  106.0 7.8 %collective-permute-start.3 = (f32[1,128,256]{2,1,0:T(8,128)S(1)}, f32[1,128,256]{2,1,0:T(8,128)S(1)}, u32[]{:S(2)}, u32[]{:S(2)}) collective-permute-start(f32[1,128,256]{2,1,0:T(8,128)S(1)} %get-tuple-element.46), channel_id=1, source_target_pairs={{8,0},{16,8},{24,16},{32,24},{40,32},{48,40},{56,48},{64,56},{72,6... | collective-permute-start | bytes 393224 | tf_op jit(solution)/shard_map/ppermute | solution.py:22
  113.9 1.9 collective-permute-start.4
  115.8 0.0 collective-permute-done.3
  115.8 7.1 %collective-permute-done.4 = f32[1,128,256]{2,1,0:T(8,128)S(1)} collective-permute-done((f32[1,128,256]{2,1,0:T(8,128)S(1)}, f32[1,128,256]{2,1,0:T(8,128)S(1)}, u32[]{:S(2)}, u32[]{:S(2)}) %collective-permute-start.4) | collective-permute-done | bytes 131104 | tf_op jit(solution)/shard_map/ppermute | solution.py:19
  122.9 1.2 fusion.33
  124.1 0.2 fusion.50
  124.3 0.2 fusion.53
  124.5 0.4 fusion.51
  124.9 1.9 collective-permute-start.5
  126.8 3.4 %collective-permute-start.6 = (f32[1,128,256]{2,1,0:T(8,128)S(1)}, f32[1,128,256]{2,1,0:T(8,128)S(1)}, u32[]{:S(2)}, u32[]{:S(2)}) collective-permute-start(f32[1,128,256]{2,1,0:T(8,128)S(1)} %get-tuple-element.37), channel_id=1, source_target_pairs={{0,8},{8,16},{16,24},{24,32},{32,40},{40,48},{48,56},{56,64},{64,7... | collective-permute-start | bytes 393224 | tf_op jit(solution)/shard_map/ppermute | solution.py:19
  130.2 0.4 collective-permute-done.5
  130.6 5.2 %collective-permute-done.6 = f32[1,128,256]{2,1,0:T(8,128)S(1)} collective-permute-done((f32[1,128,256]{2,1,0:T(8,128)S(1)}, f32[1,128,256]{2,1,0:T(8,128)S(1)}, u32[]{:S(2)}, u32[]{:S(2)}) %collective-permute-start.6) | collective-permute-done | bytes 131104 | tf_op jit(solution)/shard_map/ppermute | solution.py:19
  135.9 1.2 fusion.25
  137.1 0.2 fusion.45
  137.3 0.2 fusion.48
  137.5 0.4 fusion.46
  137.9 1.9 collective-permute-start.7
  139.8 3.4 %collective-permute-start.8 = (f32[1,128,256]{2,1,0:T(8,128)S(1)}, f32[1,128,256]{2,1,0:T(8,128)S(1)}, u32[]{:S(2)}, u32[]{:S(2)}) collective-permute-start(f32[1,128,256]{2,1,0:T(8,128)S(1)} %get-tuple-element.27), channel_id=1, source_target_pairs={{0,8},{8,16},{16,24},{24,32},{32,40},{40,48},{48,56},{56,64},{64,7... | collective-permute-start | bytes 393224 | tf_op jit(solution)/shard_map/ppermute | solution.py:19
  143.2 0.4 collective-permute-done.7
  143.6 5.2 %collective-permute-done.8 = f32[1,128,256]{2,1,0:T(8,128)S(1)} collective-permute-done((f32[1,128,256]{2,1,0:T(8,128)S(1)}, f32[1,128,256]{2,1,0:T(8,128)S(1)}, u32[]{:S(2)}, u32[]{:S(2)}) %collective-permute-start.8) | collective-permute-done | bytes 131104 | tf_op jit(solution)/shard_map/ppermute | solution.py:19
  148.8 1.2 fusion.17
  150.1 0.0 copy-start.1
  150.1 0.2 fusion.40
  150.3 0.2 fusion.43
  150.5 0.4 fusion.41
  150.9 1.9 collective-permute-start.9
  152.8 3.4 %collective-permute-start.10 = (f32[1,128,256]{2,1,0:T(8,128)S(1)}, f32[1,128,256]{2,1,0:T(8,128)S(1)}, u32[]{:S(2)}, u32[]{:S(2)}) collective-permute-start(f32[1,128,256]{2,1,0:T(8,128)S(1)} %get-tuple-element.17), channel_id=1, source_target_pairs={{0,8},{8,16},{16,24},{24,32},{32,40},{40,48},{48,56},{56,64},{64,7... | collective-permute-start | bytes 393224 | tf_op jit(solution)/shard_map/ppermute | solution.py:19
  156.2 0.4 collective-permute-done.9
  156.6 5.2 %collective-permute-done.10 = f32[1,128,256]{2,1,0:T(8,128)S(1)} collective-permute-done((f32[1,128,256]{2,1,0:T(8,128)S(1)}, f32[1,128,256]{2,1,0:T(8,128)S(1)}, u32[]{:S(2)}, u32[]{:S(2)}) %collective-permute-start.10) | collective-permute-done | bytes 131104 | tf_op jit(solution)/shard_map/ppermute | solution.py:19
  161.8 0.0 copy-done.1
  161.8 2.4 %fusion.2 = f32[8,128,256]{2,1,0:T(8,128)} fusion(f32[8,128,256]{2,1,0:T(8,128)S(1)} %fusion.17, f32[1,128,256]{2,1,0:T(8,128)S(1)} %collective-permute-done.10, f32[1,128,256]{2,1,0:T(8,128)S(1)} %collective-permute-done.9, f32[8,1,256]{2,1,0:T(1,128)S(1)} %get-tuple-element.13, f32[8,127,256]{2,1,0:T(8,128)S(1)} %get-tuple-element.15, ...), kind=kLoop, calls=%fused_computation.6 | loop fusion | flops 4980736 | bytes 6553604 | tf_op jit(solution)/shard_map/mul | solution.py:98
  164.2 0.0 all-reduce.2.cloned.1.call-update
  164.3 55.1 %all-reduce.2.cloned.1.call-done = f32[8,128,256]{2,1,0:T(8,128)} async-done(((f32[8,128,256]{2,1,0:T(8,128)}), f32[8,128,256]{2,1,0:T(8,128)}) %all-reduce.2.cloned.1.call-update) | async-done | bytes 1048592 | tf_op jit(solution)/shard_map/psum | solution.py:98
  219.4 2.4 %add_bitcast_fusion = f32[1,8,128,256]{3,2,1,0:T(8,128)} fusion(f32[8,128,256]{2,1,0:T(8,128)} %all-reduce.2.cloned.1.call-done, f32[8,128,256]{2,1,0:T(8,128)S(1)} %collective-permute-done.2, f32[1,8,128,256]{3,2,1,0:T(8,128)S(1)} %copy-done.2, pred[]{:T(512)S(6)} %eq.3), kind=kLoop, calls=%fused_computation.55 | loop fusion | flops 786432 | bytes 4194305 | tf_op jit(solution)/shard_map/broadcast_in_dim | solution.py:100
  (11 shorter events, 0.2 us)
Async XLA Ops:
  7.2 20.5 %copy-start = (f32[1,1,8,128,256]{4,3,2,1,0:T(8,128)S(1)}, f32[1,1,8,128,256]{4,3,2,1,0:T(8,128)}, u32[]{:S(2)}) copy-start(f32[1,1,8,128,256]{4,3,2,1,0:T(8,128)} %param.6) | copy-start | bytes 3145732
  7.2 65.7 %all-gather.3.cloned.1.call-start = ((), (), s32[]{:S(2)}) async-start(), calls=%async_computation.1 | async-start | bytes 5242880 | tf_op jit(solution)/shard_map/all_gather | solution.py:83
  8.3 19.6 %collective-permute-start = (f32[1,128,256]{2,1,0:T(8,128)S(1)}, f32[1,128,256]{2,1,0:T(8,128)S(1)}, u32[]{:S(2)}, u32[]{:S(2)}) collective-permute-start(f32[1,128,256]{2,1,0:T(8,128)S(1)} %get-tuple-element.48), channel_id=1, source_target_pairs={{8,0},{16,8},{24,16},{32,24},{40,32},{48,40},{56,48},{64,56},{72,6... | collective-permute-start | bytes 393224 | tf_op jit(solution)/shard_map/ppermute | solution.py:22
  22.4 9.0 %collective-permute-start.1 = (f32[1,128,256]{2,1,0:T(8,128)S(1)}, f32[1,128,256]{2,1,0:T(8,128)S(1)}, u32[]{:S(2)}, u32[]{:S(2)}) collective-permute-start(f32[1,128,256]{2,1,0:T(8,128)S(1)} %get-tuple-element.49), channel_id=1, source_target_pairs={{0,8},{8,16},{16,24},{24,32},{32,40},{40,48},{48,56},{56,64},{64,7... | collective-permute-start | bytes 393224 | tf_op jit(solution)/shard_map/ppermute | solution.py:19
  31.5 41.4 %copy-start.3 = (f32[4]{0:T(128)S(1)}, f32[4]{0:T(128)}, u32[]{:S(2)}) copy-start(f32[4]{0:T(128)} %constant.30.clone) | copy-start | bytes 52
  33.7 43.2 %copy-start.2 = (f32[1,8,128,256]{3,2,1,0:T(8,128)S(1)}, f32[1,8,128,256]{3,2,1,0:T(8,128)}, u32[]{:S(2)}) copy-start(f32[1,8,128,256]{3,2,1,0:T(8,128)} %param.5) | copy-start | bytes 3145732
  33.7 185.7 %all-reduce.2.cloned.1.call-start = ((), (), s32[]{:S(2)}) async-start(), calls=%async_computation | async-start | bytes 2097152 | tf_op jit(solution)/shard_map/psum | solution.py:98
  72.8 8.1 %copy-start.4 = (f32[4]{0:T(128)S(1)}, f32[4]{0:T(128)}, u32[]{:S(2)}) copy-start(f32[4]{0:T(128)} %constant.29.clone) | copy-start | bytes 52
  78.0 24.7 %collective-permute-start.2 = (f32[8,128,256]{2,1,0:T(8,128)}, f32[8,128,256]{2,1,0:T(8,128)S(1)}, u32[]{:S(2)}, u32[]{:S(2)}) collective-permute-start(f32[8,128,256]{2,1,0:T(8,128)} %bitcast_add_fusion), channel_id=1, source_target_pairs={{0,1},{2,3},{4,5},{6,7},{8,9},{10,11},{12,13},{14,15},{16,17},{18,... | collective-permute-start | bytes 3145736 | tf_op jit(solution)/shard_map/ppermute | solution.py:30
  106.0 9.8 %collective-permute-start.3 = (f32[1,128,256]{2,1,0:T(8,128)S(1)}, f32[1,128,256]{2,1,0:T(8,128)S(1)}, u32[]{:S(2)}, u32[]{:S(2)}) collective-permute-start(f32[1,128,256]{2,1,0:T(8,128)S(1)} %get-tuple-element.46), channel_id=1, source_target_pairs={{8,0},{16,8},{24,16},{32,24},{40,32},{48,40},{56,48},{64,56},{72,6... | collective-permute-start | bytes 393224 | tf_op jit(solution)/shard_map/ppermute | solution.py:22
  113.9 9.0 %collective-permute-start.4 = (f32[1,128,256]{2,1,0:T(8,128)S(1)}, f32[1,128,256]{2,1,0:T(8,128)S(1)}, u32[]{:S(2)}, u32[]{:S(2)}) collective-permute-start(f32[1,128,256]{2,1,0:T(8,128)S(1)} %get-tuple-element.47), channel_id=1, source_target_pairs={{0,8},{8,16},{16,24},{24,32},{32,40},{40,48},{48,56},{56,64},{64,7... | collective-permute-start | bytes 393224 | tf_op jit(solution)/shard_map/ppermute | solution.py:19
  124.9 5.7 %collective-permute-start.5 = (f32[1,128,256]{2,1,0:T(8,128)S(1)}, f32[1,128,256]{2,1,0:T(8,128)S(1)}, u32[]{:S(2)}, u32[]{:S(2)}) collective-permute-start(f32[1,128,256]{2,1,0:T(8,128)S(1)} %get-tuple-element.36), channel_id=1, source_target_pairs={{8,0},{16,8},{24,16},{32,24},{40,32},{48,40},{56,48},{64,56},{72,6... | collective-permute-start | bytes 393224 | tf_op jit(solution)/shard_map/ppermute | solution.py:22
  126.8 9.0 %collective-permute-start.6 = (f32[1,128,256]{2,1,0:T(8,128)S(1)}, f32[1,128,256]{2,1,0:T(8,128)S(1)}, u32[]{:S(2)}, u32[]{:S(2)}) collective-permute-start(f32[1,128,256]{2,1,0:T(8,128)S(1)} %get-tuple-element.37), channel_id=1, source_target_pairs={{0,8},{8,16},{16,24},{24,32},{32,40},{40,48},{48,56},{56,64},{64,7... | collective-permute-start | bytes 393224 | tf_op jit(solution)/shard_map/ppermute | solution.py:19
  137.9 5.7 %collective-permute-start.7 = (f32[1,128,256]{2,1,0:T(8,128)S(1)}, f32[1,128,256]{2,1,0:T(8,128)S(1)}, u32[]{:S(2)}, u32[]{:S(2)}) collective-permute-start(f32[1,128,256]{2,1,0:T(8,128)S(1)} %get-tuple-element.26), channel_id=1, source_target_pairs={{8,0},{16,8},{24,16},{32,24},{40,32},{48,40},{56,48},{64,56},{72,6... | collective-permute-start | bytes 393224 | tf_op jit(solution)/shard_map/ppermute | solution.py:22
  139.8 9.0 %collective-permute-start.8 = (f32[1,128,256]{2,1,0:T(8,128)S(1)}, f32[1,128,256]{2,1,0:T(8,128)S(1)}, u32[]{:S(2)}, u32[]{:S(2)}) collective-permute-start(f32[1,128,256]{2,1,0:T(8,128)S(1)} %get-tuple-element.27), channel_id=1, source_target_pairs={{0,8},{8,16},{16,24},{24,32},{32,40},{40,48},{48,56},{56,64},{64,7... | collective-permute-start | bytes 393224 | tf_op jit(solution)/shard_map/ppermute | solution.py:19
  150.1 11.8 %copy-start.1 = (f32[8,128,256]{2,1,0:T(8,128)}, f32[8,128,256]{2,1,0:T(8,128)S(1)}, u32[]{:S(2)}) copy-start(f32[8,128,256]{2,1,0:T(8,128)S(1)} %fusion.17) | copy-start | bytes 3145732
  150.9 5.7 %collective-permute-start.9 = (f32[1,128,256]{2,1,0:T(8,128)S(1)}, f32[1,128,256]{2,1,0:T(8,128)S(1)}, u32[]{:S(2)}, u32[]{:S(2)}) collective-permute-start(f32[1,128,256]{2,1,0:T(8,128)S(1)} %get-tuple-element.16), channel_id=1, source_target_pairs={{8,0},{16,8},{24,16},{32,24},{40,32},{48,40},{56,48},{64,56},{72,6... | collective-permute-start | bytes 393224 | tf_op jit(solution)/shard_map/ppermute | solution.py:22
  152.8 9.0 %collective-permute-start.10 = (f32[1,128,256]{2,1,0:T(8,128)S(1)}, f32[1,128,256]{2,1,0:T(8,128)S(1)}, u32[]{:S(2)}, u32[]{:S(2)}) collective-permute-start(f32[1,128,256]{2,1,0:T(8,128)S(1)} %get-tuple-element.17), channel_id=1, source_target_pairs={{0,8},{8,16},{16,24},{24,32},{32,40},{40,48},{48,56},{56,64},{64,7... | collective-permute-start | bytes 393224 | tf_op jit(solution)/shard_map/ppermute | solution.py:19
Sparse Core Ops, SparseCore 0:
  33.8 38.9 all-gather.2
  164.4 54.9 all-reduce.1
where the time goes:
time: 229 us
  waiting for transfers between devices  142 us (62%)
  starting transfers between devices  44 us (19%)
  other arithmetic  18.3 us (8%)
  between operations  14.9 us (7%)
  local copies, waits for them, and re-layouts  9.72 us (4%)
    psum x1, waiting for transfers between devices, on_device(): weighted_new = lax.psum(node_weight * force_new, 'node')  55.1 us
    all_gather x1, waiting for transfers between devices, on_device(): shard_piece = lax.all_gather(force_old[None], 'node', axis=0, tiled=True)  38.3 us
    ppermute x5, starting transfers between devices, padded_2(): lax.ppermute(lax.slice_in_dim(block, 0, width, axis=dim), axis, backward)  27.7 us
    ppermute x5, waiting for transfers between devices, padded_2(): lax.ppermute(lax.slice_in_dim(block, block.shape[dim] - width, None, axis...  26.4 us
    ppermute x1, waiting for transfers between devices, shifted_2(): return lax.ppermute(array, axis, pairs)  20.7 us
    ppermute x5, starting transfers between devices, padded_2(): lax.ppermute(lax.slice_in_dim(block, block.shape[dim] - width, None, axis...  13.9 us
    div x4, other arithmetic, on_device(): iterate = (right_side + implicit * neighbour_sum(widened)) / divisor  6.12 us
    slice x10, local copies, waits for them, and re-layouts, neighbour_sum(): total = total + jnp.roll(inner, -1, 2) + jnp.roll(inner, 1, 2)  5.54 us
  transfers between devices with their start and end apart: 13, of which 11 were waited for; matrix products, arithmetic and copies ran while one was open for 2% of the time, Pallas kernels for 0%

commit v1 on v0

--- a/solution.py
+++ b/solution.py
@@ -95,7 +95,7 @@
         iterate = (right_side + implicit * neighbour_sum(widened)) / divisor
     padded_new = padded_2(iterate, (("space", 0),), 1)
     laplace_new, force_new = forcing(iterate, padded_new)
-    weighted_new = lax.psum(node_weight * force_new, "node")
+    weighted_new = jnp.sum(lax.all_gather(node_weight * force_new, "node"), axis=0)
     end_new = begin_state + time_step * weighted_new
     return (iterate[None, None], end_new[None])
 

time: 229 us -> 216 us (0.943)
  waiting for transfers between devices: 142 us -> 127 us
    psum x1 -> x0, waiting for transfers between devices: 55.1 us -> none  [on_device(): weighted_new = lax.psum(node_weight * force_new, 'node')]
    all_gather x0 -> x1, waiting for transfers between devices: none -> 40.6 us  [on_device(): lax.all_gather(node_weight * force_new, 'node')]
    reduce_sum x0 -> x1, other arithmetic: none -> 2.6 us  [on_device(): jnp.sum(lax.all_gather(node_weight * force_new, 'node'), axis=0)]
  transfers between devices with their start and end apart: 13 -> 13, of which waited for: 11 -> 11; matrix products, arithmetic and copies ran while one was open for 2% -> 3% of each run, Pallas kernels for 0% -> 0%
where the time goes in v1:
time: 216 us; the launch traced here: 215 us
  waiting for transfers between devices  127 us (59%)
  starting transfers between devices  44 us (20%)
  other arithmetic  19.7 us (9%)
  between operations  14.9 us (7%)
  local copies, waits for them, and re-layouts  9.72 us (5%)
    all_gather x1, waiting for transfers between devices, on_device(): lax.all_gather(node_weight * force_new, 'node')  40.6 us
    all_gather x1, waiting for transfers between devices, on_device(): shard_piece = lax.all_gather(force_old[None], 'node', axis=0, tiled=True)  38.3 us
    ppermute x5, starting transfers between devices, padded_2(): lax.ppermute(lax.slice_in_dim(block, 0, width, axis=dim), axis, backward)  27.7 us
    ppermute x5, waiting for transfers between devices, padded_2(): lax.ppermute(lax.slice_in_dim(block, block.shape[dim] - width, None, axis...  26.4 us
    ppermute x1, waiting for transfers between devices, shifted_2(): return lax.ppermute(array, axis, pairs)  20.7 us
    ppermute x5, starting transfers between devices, padded_2(): lax.ppermute(lax.slice_in_dim(block, block.shape[dim] - width, None, axis...  13.9 us
    div x4, other arithmetic, on_device(): iterate = (right_side + implicit * neighbour_sum(widened)) / divisor  6.12 us
    slice x10, local copies, waits for them, and re-layouts, neighbour_sum(): total = total + jnp.roll(inner, -1, 2) + jnp.roll(inner, 1, 2)  5.53 us
  transfers between devices with their start and end apart: 13, of which 11 were waited for; matrix products, arithmetic and copies ran while one was open for 3% of the time, Pallas kernels for 0%

profile of v1, /device:TPU:1, one launch (start us, length us, event | category | flops | bytes accessed | tf_op | source)
XLA Modules:
  0.0 215.5 jit_solution(17102169346021528165)
XLA Ops:
  7.2 0.0 copy-start
  7.2 0.0 all-gather.5.cloned.1.call-start
  7.2 1.1 slice_bitcast_fusion.1
  8.3 14.1 %collective-permute-start = (f32[1,128,256]{2,1,0:T(8,128)S(1)}, f32[1,128,256]{2,1,0:T(8,128)S(1)}, u32[]{:S(2)}, u32[]{:S(2)}) collective-permute-start(f32[1,128,256]{2,1,0:T(8,128)S(1)} %get-tuple-element.48), channel_id=1, source_target_pairs={{8,0},{16,8},{24,16},{32,24},{40,32},{48,40},{56,48},{64,56},{72,6... | collective-permute-start | bytes 393224 | tf_op jit(solution)/shard_map/ppermute | solution.py:22
  22.4 1.9 collective-permute-start.1
  24.4 1.4 fusion.63
  25.8 1.9 fusion.62
  27.7 0.0 copy-done
  27.7 0.2 fusion.60
  27.9 0.0 collective-permute-done
  27.9 3.6 %collective-permute-done.1 = f32[1,128,256]{2,1,0:T(8,128)S(1)} collective-permute-done((f32[1,128,256]{2,1,0:T(8,128)S(1)}, f32[1,128,256]{2,1,0:T(8,128)S(1)}, u32[]{:S(2)}, u32[]{:S(2)}) %collective-permute-start.1) | collective-permute-done | bytes 131104 | tf_op jit(solution)/shard_map/ppermute | solution.py:19
  31.5 2.2 %fusion = (f32[8,128,256]{2,1,0:T(8,128)}, f32[8,128,256]{2,1,0:T(8,128)}) fusion(f32[1,1,8,128,256]{4,3,2,1,0:T(8,128)S(1)} %copy-done, f32[8,128,255]{2,1,0:T(8,128)S(1)} %get-tuple-element.55, f32[8,128,1]{2,1,0:T(8,128)S(1)} %get-tuple-element.57, f32[8,128,1]{2,1,0:T(8,128)S(1)} %get-tuple-element.56, f32[8,128,255]{2,1,0:T(8,128)S(1)} %get-tuple-element.54, ...), kind=kLoop, calls=%fused_computation.4 | loop fusion | flops 4718592 | bytes 8650752 | tf_op jit(solution)/shard_map/add | solution.py:68
  33.7 0.0 all-gather.5.cloned.1.call-update
  33.7 0.0 all-gather.7.cloned.1.call-start
  33.8 0.8 dynamic-slice_bitcast_fusion
  34.5 38.3 %all-gather.5.cloned.1.call-done = f32[32,128,256]{2,1,0:T(8,128)} async-done(((f32[8,128,256]{2,1,0:T(8,128)}), f32[32,128,256]{2,1,0:T(8,128)}) %all-gather.5.cloned.1.call-update) | async-done | bytes 4194320 | tf_op jit(solution)/shard_map/all_gather | solution.py:83
  72.8 0.0 copy-done.3
  72.9 4.1 %multiply_reduce_fusion.1 = (f32[8,128,256]{2,1,0:T(8,128)S(1)}, f32[8,128,256]{2,1,0:T(8,128)}) fusion(f32[4,8,128,256]{3,2,1,0:T(8,128)} %bitcast.31, f32[4]{0:T(128)S(1)} %copy-done.3, f32[4]{0:T(128)S(1)} %dynamic-slice_bitcast_fusion), kind=kLoop, calls=%fused_computation.1 | loop fusion | flops 3670016 | bytes 6291488 | tf_op jit(solution)/shard_map/reduce_sum | solution.py:85
  76.9 0.0 copy-done.2
  76.9 1.1 bitcast_add_fusion
  78.0 2.3 %collective-permute-start.2 = (f32[8,128,256]{2,1,0:T(8,128)}, f32[8,128,256]{2,1,0:T(8,128)S(1)}, u32[]{:S(2)}, u32[]{:S(2)}) collective-permute-start(f32[8,128,256]{2,1,0:T(8,128)} %bitcast_add_fusion), channel_id=1, source_target_pairs={{0,1},{2,3},{4,5},{6,7},{8,9},{10,11},{12,13},{14,15},{16,17},{18,... | collective-permute-start | bytes 3145736 | tf_op jit(solution)/shard_map/ppermute | solution.py:30
  80.3 0.7 dynamic_slice.11
  81.0 0.0 copy-done.4
  81.0 0.6 dynamic_slice.10
  82.1 20.7 %collective-permute-done.2 = f32[8,128,256]{2,1,0:T(8,128)S(1)} collective-permute-done((f32[8,128,256]{2,1,0:T(8,128)}, f32[8,128,256]{2,1,0:T(8,128)S(1)}, u32[]{:S(2)}, u32[]{:S(2)}) %collective-permute-start.2) | collective-permute-done | bytes 1048608 | tf_op jit(solution)/shard_map/ppermute | solution.py:30
  102.8 2.5 %add_divide_fusion = (f32[8,128,256]{2,1,0:T(8,128)S(1)}, f32[8,128,256]{2,1,0:T(8,128)S(1)}) fusion(f32[8,128,256]{2,1,0:T(8,128)} %get-tuple-element.7, f32[]{:T(128)S(6)} %add.125, f32[]{:T(128)} %bitcast.6, f32[1,1,8,128,256]{4,3,2,1,0:T(8,128)S(1)} %copy-done, f32[8,128,256]{2,1,0:T(8,128)} %get-tuple-element.3, ...), kind=kLoop, calls=%fused_computation.56 | loop fusion | flops 2621440 | bytes 7340041 | tf_op jit(solution)/shard_map/div | solution.py:95
  105.3 0.2 fusion.55
  105.5 0.2 fusion.58
  105.7 0.4 fusion.56
  106.0 7.8 %collective-permute-start.3 = (f32[1,128,256]{2,1,0:T(8,128)S(1)}, f32[1,128,256]{2,1,0:T(8,128)S(1)}, u32[]{:S(2)}, u32[]{:S(2)}) collective-permute-start(f32[1,128,256]{2,1,0:T(8,128)S(1)} %get-tuple-element.46), channel_id=1, source_target_pairs={{8,0},{16,8},{24,16},{32,24},{40,32},{48,40},{56,48},{64,56},{72,6... | collective-permute-start | bytes 393224 | tf_op jit(solution)/shard_map/ppermute | solution.py:22
  113.9 1.9 collective-permute-start.4
  115.8 0.0 collective-permute-done.3
  115.8 7.1 %collective-permute-done.4 = f32[1,128,256]{2,1,0:T(8,128)S(1)} collective-permute-done((f32[1,128,256]{2,1,0:T(8,128)S(1)}, f32[1,128,256]{2,1,0:T(8,128)S(1)}, u32[]{:S(2)}, u32[]{:S(2)}) %collective-permute-start.4) | collective-permute-done | bytes 131104 | tf_op jit(solution)/shard_map/ppermute | solution.py:19
  122.9 1.2 fusion.33
  124.1 0.2 fusion.50
  124.3 0.2 fusion.53
  124.5 0.4 fusion.51
  124.9 1.9 collective-permute-start.5
  126.8 3.4 %collective-permute-start.6 = (f32[1,128,256]{2,1,0:T(8,128)S(1)}, f32[1,128,256]{2,1,0:T(8,128)S(1)}, u32[]{:S(2)}, u32[]{:S(2)}) collective-permute-start(f32[1,128,256]{2,1,0:T(8,128)S(1)} %get-tuple-element.37), channel_id=1, source_target_pairs={{0,8},{8,16},{16,24},{24,32},{32,40},{40,48},{48,56},{56,64},{64,7... | collective-permute-start | bytes 393224 | tf_op jit(solution)/shard_map/ppermute | solution.py:19
  130.2 0.4 collective-permute-done.5
  130.6 5.2 %collective-permute-done.6 = f32[1,128,256]{2,1,0:T(8,128)S(1)} collective-permute-done((f32[1,128,256]{2,1,0:T(8,128)S(1)}, f32[1,128,256]{2,1,0:T(8,128)S(1)}, u32[]{:S(2)}, u32[]{:S(2)}) %collective-permute-start.6) | collective-permute-done | bytes 131104 | tf_op jit(solution)/shard_map/ppermute | solution.py:19
  135.9 1.2 fusion.25
  137.1 0.2 fusion.45
  137.3 0.2 fusion.48
  137.5 0.4 fusion.46
  137.9 1.9 collective-permute-start.7
  139.8 3.4 %collective-permute-start.8 = (f32[1,128,256]{2,1,0:T(8,128)S(1)}, f32[1,128,256]{2,1,0:T(8,128)S(1)}, u32[]{:S(2)}, u32[]{:S(2)}) collective-permute-start(f32[1,128,256]{2,1,0:T(8,128)S(1)} %get-tuple-element.27), channel_id=1, source_target_pairs={{0,8},{8,16},{16,24},{24,32},{32,40},{40,48},{48,56},{56,64},{64,7... | collective-permute-start | bytes 393224 | tf_op jit(solution)/shard_map/ppermute | solution.py:19
  143.2 0.4 collective-permute-done.7
  143.6 5.2 %collective-permute-done.8 = f32[1,128,256]{2,1,0:T(8,128)S(1)} collective-permute-done((f32[1,128,256]{2,1,0:T(8,128)S(1)}, f32[1,128,256]{2,1,0:T(8,128)S(1)}, u32[]{:S(2)}, u32[]{:S(2)}) %collective-permute-start.8) | collective-permute-done | bytes 131104 | tf_op jit(solution)/shard_map/ppermute | solution.py:19
  148.8 1.2 fusion.17
  150.1 0.0 copy-start.1
  150.1 0.2 fusion.40
  150.3 0.2 fusion.43
  150.5 0.4 fusion.41
  150.9 1.9 collective-permute-start.9
  152.8 3.4 %collective-permute-start.10 = (f32[1,128,256]{2,1,0:T(8,128)S(1)}, f32[1,128,256]{2,1,0:T(8,128)S(1)}, u32[]{:S(2)}, u32[]{:S(2)}) collective-permute-start(f32[1,128,256]{2,1,0:T(8,128)S(1)} %get-tuple-element.17), channel_id=1, source_target_pairs={{0,8},{8,16},{16,24},{24,32},{32,40},{40,48},{48,56},{56,64},{64,7... | collective-permute-start | bytes 393224 | tf_op jit(solution)/shard_map/ppermute | solution.py:19
  156.2 0.4 collective-permute-done.9
  156.6 5.2 %collective-permute-done.10 = f32[1,128,256]{2,1,0:T(8,128)S(1)} collective-permute-done((f32[1,128,256]{2,1,0:T(8,128)S(1)}, f32[1,128,256]{2,1,0:T(8,128)S(1)}, u32[]{:S(2)}, u32[]{:S(2)}) %collective-permute-start.10) | collective-permute-done | bytes 131104 | tf_op jit(solution)/shard_map/ppermute | solution.py:19
  161.8 0.0 copy-done.1
  161.8 2.4 %fusion.2 = f32[8,128,256]{2,1,0:T(8,128)} fusion(f32[8,128,256]{2,1,0:T(8,128)S(1)} %fusion.17, f32[1,128,256]{2,1,0:T(8,128)S(1)} %collective-permute-done.10, f32[1,128,256]{2,1,0:T(8,128)S(1)} %collective-permute-done.9, f32[8,1,256]{2,1,0:T(1,128)S(1)} %get-tuple-element.13, f32[8,127,256]{2,1,0:T(8,128)S(1)} %get-tuple-element.15, ...), kind=kLoop, calls=%fused_computation.6 | loop fusion | flops 4980736 | bytes 6553604 | tf_op jit(solution)/shard_map/mul | solution.py:98
  164.2 0.0 all-gather.7.cloned.1.call-update
  164.3 40.6 %all-gather.7.cloned.1.call-done = f32[32,128,256]{2,1,0:T(8,128)} async-done(((f32[8,128,256]{2,1,0:T(8,128)}), f32[32,128,256]{2,1,0:T(8,128)}) %all-gather.7.cloned.1.call-update) | async-done | bytes 4194320 | tf_op jit(solution)/shard_map/all_gather | solution.py:98
  204.9 2.6 %reduce_sum.29 = f32[8,128,256]{2,1,0:T(8,128)S(1)} reduce(f32[4,8,128,256]{3,2,1,0:T(8,128)} %bitcast.32, f32[]{:T(128)} %constant.8.clone.1), dimensions={0}, to_apply=%region_2.3 | reduce | flops 786432 | bytes 5242884 | tf_op jit(solution)/shard_map/reduce_sum | solution.py:98
  207.5 1.2 add_bitcast_fusion
  (12 shorter events, 0.2 us)
Async XLA Ops:
  7.2 20.5 %copy-start = (f32[1,1,8,128,256]{4,3,2,1,0:T(8,128)S(1)}, f32[1,1,8,128,256]{4,3,2,1,0:T(8,128)}, u32[]{:S(2)}) copy-start(f32[1,1,8,128,256]{4,3,2,1,0:T(8,128)} %param.6) | copy-start | bytes 3145732
  7.2 65.7 %all-gather.5.cloned.1.call-start = ((), (), s32[]{:S(2)}) async-start(), calls=%async_computation | async-start | bytes 5242880 | tf_op jit(solution)/shard_map/all_gather | solution.py:83
  8.3 19.6 %collective-permute-start = (f32[1,128,256]{2,1,0:T(8,128)S(1)}, f32[1,128,256]{2,1,0:T(8,128)S(1)}, u32[]{:S(2)}, u32[]{:S(2)}) collective-permute-start(f32[1,128,256]{2,1,0:T(8,128)S(1)} %get-tuple-element.48), channel_id=1, source_target_pairs={{8,0},{16,8},{24,16},{32,24},{40,32},{48,40},{56,48},{64,56},{72,6... | collective-permute-start | bytes 393224 | tf_op jit(solution)/shard_map/ppermute | solution.py:22
  22.4 9.0 %collective-permute-start.1 = (f32[1,128,256]{2,1,0:T(8,128)S(1)}, f32[1,128,256]{2,1,0:T(8,128)S(1)}, u32[]{:S(2)}, u32[]{:S(2)}) collective-permute-start(f32[1,128,256]{2,1,0:T(8,128)S(1)} %get-tuple-element.49), channel_id=1, source_target_pairs={{0,8},{8,16},{16,24},{24,32},{32,40},{40,48},{48,56},{56,64},{64,7... | collective-permute-start | bytes 393224 | tf_op jit(solution)/shard_map/ppermute | solution.py:19
  31.5 41.4 %copy-start.3 = (f32[4]{0:T(128)S(1)}, f32[4]{0:T(128)}, u32[]{:S(2)}) copy-start(f32[4]{0:T(128)} %constant.30.clone) | copy-start | bytes 52
  33.7 43.2 %copy-start.2 = (f32[1,8,128,256]{3,2,1,0:T(8,128)S(1)}, f32[1,8,128,256]{3,2,1,0:T(8,128)}, u32[]{:S(2)}) copy-start(f32[1,8,128,256]{3,2,1,0:T(8,128)} %param.5) | copy-start | bytes 3145732
  33.7 171.2 %all-gather.7.cloned.1.call-start = ((), (), s32[]{:S(2)}) async-start(), calls=%async_computation.1 | async-start | bytes 5242880 | tf_op jit(solution)/shard_map/all_gather | solution.py:98
  72.9 8.1 %copy-start.4 = (f32[4]{0:T(128)S(1)}, f32[4]{0:T(128)}, u32[]{:S(2)}) copy-start(f32[4]{0:T(128)} %constant.29.clone) | copy-start | bytes 52
  78.0 24.7 %collective-permute-start.2 = (f32[8,128,256]{2,1,0:T(8,128)}, f32[8,128,256]{2,1,0:T(8,128)S(1)}, u32[]{:S(2)}, u32[]{:S(2)}) collective-permute-start(f32[8,128,256]{2,1,0:T(8,128)} %bitcast_add_fusion), channel_id=1, source_target_pairs={{0,1},{2,3},{4,5},{6,7},{8,9},{10,11},{12,13},{14,15},{16,17},{18,... | collective-permute-start | bytes 3145736 | tf_op jit(solution)/shard_map/ppermute | solution.py:30
  106.0 9.8 %collective-permute-start.3 = (f32[1,128,256]{2,1,0:T(8,128)S(1)}, f32[1,128,256]{2,1,0:T(8,128)S(1)}, u32[]{:S(2)}, u32[]{:S(2)}) collective-permute-start(f32[1,128,256]{2,1,0:T(8,128)S(1)} %get-tuple-element.46), channel_id=1, source_target_pairs={{8,0},{16,8},{24,16},{32,24},{40,32},{48,40},{56,48},{64,56},{72,6... | collective-permute-start | bytes 393224 | tf_op jit(solution)/shard_map/ppermute | solution.py:22
  113.9 9.0 %collective-permute-start.4 = (f32[1,128,256]{2,1,0:T(8,128)S(1)}, f32[1,128,256]{2,1,0:T(8,128)S(1)}, u32[]{:S(2)}, u32[]{:S(2)}) collective-permute-start(f32[1,128,256]{2,1,0:T(8,128)S(1)} %get-tuple-element.47), channel_id=1, source_target_pairs={{0,8},{8,16},{16,24},{24,32},{32,40},{40,48},{48,56},{56,64},{64,7... | collective-permute-start | bytes 393224 | tf_op jit(solution)/shard_map/ppermute | solution.py:19
  124.9 5.7 %collective-permute-start.5 = (f32[1,128,256]{2,1,0:T(8,128)S(1)}, f32[1,128,256]{2,1,0:T(8,128)S(1)}, u32[]{:S(2)}, u32[]{:S(2)}) collective-permute-start(f32[1,128,256]{2,1,0:T(8,128)S(1)} %get-tuple-element.36), channel_id=1, source_target_pairs={{8,0},{16,8},{24,16},{32,24},{40,32},{48,40},{56,48},{64,56},{72,6... | collective-permute-start | bytes 393224 | tf_op jit(solution)/shard_map/ppermute | solution.py:22
  126.8 9.0 %collective-permute-start.6 = (f32[1,128,256]{2,1,0:T(8,128)S(1)}, f32[1,128,256]{2,1,0:T(8,128)S(1)}, u32[]{:S(2)}, u32[]{:S(2)}) collective-permute-start(f32[1,128,256]{2,1,0:T(8,128)S(1)} %get-tuple-element.37), channel_id=1, source_target_pairs={{0,8},{8,16},{16,24},{24,32},{32,40},{40,48},{48,56},{56,64},{64,7... | collective-permute-start | bytes 393224 | tf_op jit(solution)/shard_map/ppermute | solution.py:19
  137.9 5.7 %collective-permute-start.7 = (f32[1,128,256]{2,1,0:T(8,128)S(1)}, f32[1,128,256]{2,1,0:T(8,128)S(1)}, u32[]{:S(2)}, u32[]{:S(2)}) collective-permute-start(f32[1,128,256]{2,1,0:T(8,128)S(1)} %get-tuple-element.26), channel_id=1, source_target_pairs={{8,0},{16,8},{24,16},{32,24},{40,32},{48,40},{56,48},{64,56},{72,6... | collective-permute-start | bytes 393224 | tf_op jit(solution)/shard_map/ppermute | solution.py:22
  139.8 9.0 %collective-permute-start.8 = (f32[1,128,256]{2,1,0:T(8,128)S(1)}, f32[1,128,256]{2,1,0:T(8,128)S(1)}, u32[]{:S(2)}, u32[]{:S(2)}) collective-permute-start(f32[1,128,256]{2,1,0:T(8,128)S(1)} %get-tuple-element.27), channel_id=1, source_target_pairs={{0,8},{8,16},{16,24},{24,32},{32,40},{40,48},{48,56},{56,64},{64,7... | collective-permute-start | bytes 393224 | tf_op jit(solution)/shard_map/ppermute | solution.py:19
  150.1 11.8 %copy-start.1 = (f32[8,128,256]{2,1,0:T(8,128)}, f32[8,128,256]{2,1,0:T(8,128)S(1)}, u32[]{:S(2)}) copy-start(f32[8,128,256]{2,1,0:T(8,128)S(1)} %fusion.17) | copy-start | bytes 3145732
  150.9 5.7 %collective-permute-start.9 = (f32[1,128,256]{2,1,0:T(8,128)S(1)}, f32[1,128,256]{2,1,0:T(8,128)S(1)}, u32[]{:S(2)}, u32[]{:S(2)}) collective-permute-start(f32[1,128,256]{2,1,0:T(8,128)S(1)} %get-tuple-element.16), channel_id=1, source_target_pairs={{8,0},{16,8},{24,16},{32,24},{40,32},{48,40},{56,48},{64,56},{72,6... | collective-permute-start | bytes 393224 | tf_op jit(solution)/shard_map/ppermute | solution.py:22
  152.8 9.0 %collective-permute-start.10 = (f32[1,128,256]{2,1,0:T(8,128)S(1)}, f32[1,128,256]{2,1,0:T(8,128)S(1)}, u32[]{:S(2)}, u32[]{:S(2)}) collective-permute-start(f32[1,128,256]{2,1,0:T(8,128)S(1)} %get-tuple-element.17), channel_id=1, source_target_pairs={{0,8},{8,16},{16,24},{24,32},{32,40},{40,48},{48,56},{56,64},{64,7... | collective-permute-start | bytes 393224 | tf_op jit(solution)/shard_map/ppermute | solution.py:19
Sparse Core Ops, SparseCore 0:
  33.8 38.9 all-gather.4
  164.4 40.4 all-gather.6
